TPU v7x, 32 devices: a whole 2x2x4 slice. The times are simulated.
32 devices in a mesh: tm: 8 (over y, x, core), grp: 4 (over z).
Axes of the slice: x: 2, y: 2, z: 4, core: 2. Of those that a mesh axis runs over, the one named last changes fastest.
Arguments:
- series: float32 [131072, 512], P(('tm', 'grp')), may hold values from -6 to 6
- filter_taps: float32 [33], replicated, may hold values from -1 to 1
- sign_flips: int32 [131072], P(('tm', 'grp')), may hold values from -1 to 1, as said below
- samples: int32 [8192], replicated, may hold values from 0 to 131071, as said below
Outputs:
- sketch: float32 [8192, 512], P(('tm', 'grp'))
- r_factor: float32 [512, 512], replicated
Inputs may be any that keep to these rules, and one draw needn't show every extreme that they name: `sign_flips`: each entry is -1 or +1. All distinct; the values of samples modulo 4096 take exactly 4096 distinct values, each by exactly 2 consecutive entries; entries are ordered by their value modulo 4096, then by value.
All inputs are finite; a program needn't handle non-finite values.
Results may differ from a plain program's by a relative error of at most 0.0003.
Values sent between devices are 32-bit elements; how exact they have to be, the bound alone decides.
A program may use at most 128 MiB of HBM per device.

v0:
```python
import jax
import jax.numpy as jnp
from jax import lax
from jax.sharding import PartitionSpec as P


def extended(block, sides, width):
    for axis, dim in sides:
        count = lax.axis_size(axis)
        forward = [(i, i + 1) for i in range(count - 1)]
        backward = [(target, source) for source, target in forward]
        low = lax.ppermute(
            lax.slice_in_dim(block, block.shape[dim] - width, None, axis=dim), axis, forward
        )
        high = lax.ppermute(lax.slice_in_dim(block, 0, width, axis=dim), axis, backward)
        block = jnp.concatenate([low, block, high], axis=dim)
    return block


def bit_count(values, width_bits):
    counted = jnp.zeros_like(values)
    for offset in range(width_bits):
        counted = counted + (values >> offset & 1)
    return counted


def hadamard(order):
    row_ids = jnp.arange(order, dtype=jnp.int32)[:, None]
    col_ids = jnp.arange(order, dtype=jnp.int32)[None, :]
    parity = bit_count(row_ids & col_ids, max(order.bit_length(), 1)) & 1
    return (1 - 2 * parity).astype(jnp.float32)


def local_transform(rows_block):
    length, columns = rows_block.shape
    levels = length.bit_length() - 1
    outer = 2 ** ((levels + 1) // 2)
    inner = length // outer
    layered = rows_block.reshape(outer, inner, columns)
    layered = jnp.einsum("ux,xvw->uvw", hadamard(outer), layered, precision=lax.Precision.HIGHEST)
    layered = jnp.einsum("vy,uyw->uvw", hadamard(inner), layered, precision=lax.Precision.HIGHEST)
    return layered.reshape(length, columns)


def on_device(series, filter_taps, sign_flips, samples):
    rows_dev = series.shape[0]
    columns = series.shape[1]
    tap_count = filter_taps.shape[0]
    half_taps = (tap_count - 1) // 2
    devices_all = lax.axis_size("tm") * lax.axis_size("grp")
    total_rows = rows_dev * devices_all
    sample_count = samples.shape[0]
    padded = extended(series, ((("tm", "grp"), 0),), half_taps)
    filtered = filter_taps[0] * padded[0:rows_dev]
    for offset in range(1, tap_count):
        filtered = filtered + filter_taps[offset] * padded[offset : offset + rows_dev]
    flipped = filtered * sign_flips.astype(jnp.float32)[:, None]
    mixed = local_transform(flipped)
    position = lax.axis_index("tm") * lax.axis_size("grp") + lax.axis_index("grp")
    row_scale = 1.0 / jnp.sqrt(jnp.float32(total_rows))
    block_rows = sample_count // devices_all
    copies = max(2, sample_count // rows_dev)
    distinct = sample_count // copies
    per_device = distinct // devices_all
    used_positions = samples[::copies] % rows_dev
    outgoing = jnp.take(mixed, used_positions, axis=0)
    incoming = lax.all_to_all(outgoing, ("tm", "grp"), split_axis=0, concat_axis=0, tiled=True)
    stacked = incoming.reshape(devices_all, per_device, columns)
    combined = (
        jnp.einsum("op,pkw->okw", hadamard(devices_all), stacked, precision=lax.Precision.HIGHEST)
        * row_scale
    )
    combined = combined.reshape(devices_all * per_device, columns)
    mine = lax.dynamic_slice_in_dim(samples, position * block_rows, block_rows)
    slot_index = mine // rows_dev * per_device + jnp.arange(block_rows, dtype=jnp.int32) // copies
    sketch = jnp.take(combined, slot_index, axis=0)
    local_gram = lax.dot_general(
        sketch,
        sketch,
        (((0,), (0,)), ((), ())),
        precision=lax.Precision.HIGHEST,
        preferred_element_type=jnp.float32,
    )
    gram = lax.psum(local_gram, ("tm", "grp"))
    lower = jnp.linalg.cholesky(gram / sample_count)
    return (sketch, lower.T)


def solution(mesh):
    return jax.shard_map(
        on_device,
        mesh=mesh,
        in_specs=(P(("tm", "grp"), None), P(), P(("tm", "grp")), P()),
        out_specs=(P(("tm", "grp"), None), P()),
        check_vma=False,
    )
```

profile of v0, /device:TPU:0, one launch (start us, length us, event | category | flops | bytes accessed | tf_op | source)
XLA Modules:
  0.0 659.5 jit_solution(13701622514079241855)
XLA Ops:
  7.2 0.8 fusion.110
  7.9 4.9 collective-permute-start
  12.9 1.3 collective-permute-start.1
  14.2 1.4 slice.317
  15.6 2.1 fusion.111
  17.7 1.9 fusion.112
  19.6 0.7 convert_element_type.14
  20.3 0.6 constant_dynamic-update-slice_fusion.1
  20.9 11.5 %constant_dynamic-update-slice_fusion = (f32[4112,512]{1,0:T(8,128)}, f32[4112,512]{1,0:T(8,128)}) fusion(f32[4112,512]{1,0:T(8,128)} %constant_dynamic-update-slice_fusion.1, f32[4096,512]{1,0:T(8,128)} %param.4), kind=kLoop, calls=%fused_computation.143 | loop fusion | bytes 25165824 | tf_op jit(solution)/shard_map/concatenate | solution.py:16
  32.4 0.6 constant_dynamic-update-slice_fusion.2
  33.0 122.8 %fusion.1 = f32[4096,512]{1,0:T(8,128)S(1)} fusion(f32[4112,512]{1,0:T(8,128)} %constant_dynamic-update-slice_fusion.2, f32[4112,512]{1,0:T(8,128)} %get-tuple-element.10, f32[4096,512]{1,0:T(8,128)} %param.4, f32[4096]{0:T(1024)S(1)} %convert_element_type.14, f32[]{:T(128)} %bitcast.35, f32[]{:T(128)} %bitcast.34, f32[]{:T(128)} %bitcast.33, f32[]{:T(128)} %bitcast.32, ...), kind=kLoop, calls=%fused_computation.4 | loop fusion | flops 138412032 | bytes 285229184 | tf_op jit(solution)/shard_map/mul | solution.py:57
  155.8 12.4 %fusion.37 = f32[64,64,512]{2,0,1:T(8,128)S(1)} fusion(f32[64,64,512]{2,1,0:T(8,128)S(1)} %bitcast.77), kind=kOutput, calls=%fused_computation.71 | convolution fusion | flops 1610715136 | bytes 16777216 | tf_op jit(solution)/shard_map/ux,xvw->uvw/dot_general | solution.py:40
  168.3 13.8 %fusion.35 = f32[64,512,64]{1,2,0:T(8,128)} fusion(f32[64,64,512]{2,0,1:T(8,128)S(1)} %fusion.37), kind=kOutput, calls=%fused_computation.69 | convolution fusion | flops 1610715136 | bytes 16777216 | tf_op jit(solution)/shard_map/vy,uyw->uvw/dot_general | solution.py:41
  182.1 21.4 %gather_fusion = f32[4096,512]{1,0:T(8,128)} fusion(f32[4096,512]{1,0:T(8,128)} %bitcast.75, s32[4096]{0:T(1024)S(1)} %broadcast_clamp_fusion), kind=kCustom, calls=%fused_computation | custom fusion | bytes 16793600 | tf_op jit(solution)/shard_map/jit(_take)/gather | solution.py:66
  203.5 5.8 broadcast_select_fusion
  209.3 7.0 %all-to-all-start = ((f32[32,128,512]{2,1,0:T(8,128)}), f32[32,128,512]{2,1,0:T(8,128)}, u32[]{:S(2)}, u32[]{:S(2)}) async-start(f32[32,128,512]{2,1,0:T(8,128)} %broadcast_select_fusion), calls=%async_computation | async-start | bytes 16777216 | tf_op jit(solution)/shard_map/all_to_all | solution.py:67
  216.3 0.0 all-reduce.3.cloned.1.call-start
  216.4 0.8 compare_and_fusion
  217.2 180.5 %all-to-all-done = f32[32,128,512]{2,1,0:T(8,128)} async-done(((f32[32,128,512]{2,1,0:T(8,128)}), f32[32,128,512]{2,1,0:T(8,128)}, u32[]{:S(2)}, u32[]{:S(2)}) %all-to-all-start) | async-done | bytes 8388640 | tf_op jit(solution)/shard_map/all_to_all | solution.py:67
  397.7 16.9 %broadcast_multiply_fusion = f32[32,128,512]{2,0,1:T(8,128)S(1)} fusion(f32[32,128,512]{2,1,0:T(8,128)} %all-to-all-done), kind=kOutput, calls=%fused_computation.73 | convolution fusion | flops 807426048 | bytes 16777216 | tf_op jit(solution)/shard_map/op,pkw->okw/dot_general | solution.py:70
  414.6 8.1 %copy.18 = f32[32,128,512]{2,1,0:T(8,128)} copy(f32[32,128,512]{2,0,1:T(8,128)S(1)} %broadcast_multiply_fusion) | data formatting | bytes 16777216 | tf_op jit(solution)/shard_map/mul | solution.py:70
  422.7 4.6 gather_fusion.1
  427.3 0.1 broadcast_select_fusion.1
  427.4 2.0 fusion.113
  429.4 0.0 all-reduce.3.cloned.1.call-update
  429.4 134.7 %all-reduce.3.cloned.1.call-done = f32[512,512]{0,1:T(8,128)} async-done(((f32[512,512]{0,1:T(8,128)}), f32[512,512]{0,1:T(8,128)}) %all-reduce.3.cloned.1.call-update) | async-done | bytes 1048592 | tf_op jit(solution)/shard_map/psum | solution.py:84
  564.1 1.3 broadcast_multiply_fusion.1
  565.5 0.3 copy.20
  565.8 1.5 fusion.41
  567.3 11.7 %cholesky.104 = f32[128,128]{1,0:T(8,128)S(1)} custom-call(f32[128,128]{1,0:T(8,128)S(1)} %cholesky.266), custom_call_target="Cholesky" | custom-call | tf_op jit(solution)/shard_map/jit(cholesky)/cholesky | solution.py:85
  579.0 0.1 cholesky.224
  579.2 10.0 %custom-call.27 = f32[1,128,128]{1,2,0:T(8,128)S(1)} custom-call(f32[1,128,128]{2,1,0:T(8,128)S(1)} %get-tuple-element.23), custom_call_target="InvertDiagBlocksLowerTriangular" | custom-call | tf_op jit(solution)/shard_map/jit(cholesky)/cholesky | solution.py:85
  589.2 0.3 constant_dynamic-update-slice_fusion.6
  589.5 0.3 convolution_subtract_fusion
  589.8 11.7 %cholesky.217 = f32[128,128]{1,0:T(8,128)S(1)} custom-call(f32[128,128]{1,0:T(8,128)S(1)} %cholesky.270), custom_call_target="Cholesky" | custom-call | tf_op jit(solution)/shard_map/jit(cholesky)/cholesky | solution.py:85
  601.6 9.8 %custom-call.28 = f32[1,128,128]{1,2,0:T(8,128)S(1)} custom-call(f32[1,128,128]{2,1,0:T(8,128)S(1)} %get-tuple-element.20), custom_call_target="InvertDiagBlocksLowerTriangular" | custom-call | tf_op jit(solution)/shard_map/jit(cholesky)/cholesky | solution.py:85
  611.4 0.3 convolution_dynamic-update-slice_fusion
  611.7 0.4 convolution_subtract_fusion.1
  612.1 11.9 %cholesky.238 = f32[128,128]{1,0:T(8,128)S(1)} custom-call(f32[128,128]{1,0:T(8,128)S(1)} %cholesky.275), custom_call_target="Cholesky" | custom-call | tf_op jit(solution)/shard_map/jit(cholesky)/cholesky | solution.py:85
  624.0 9.8 %custom-call.29 = f32[1,128,128]{1,2,0:T(8,128)S(1)} custom-call(f32[1,128,128]{2,1,0:T(8,128)S(1)} %get-tuple-element.17), custom_call_target="InvertDiagBlocksLowerTriangular" | custom-call | tf_op jit(solution)/shard_map/jit(cholesky)/cholesky | solution.py:85
  633.9 0.2 convolution_dynamic-update-slice_fusion.1
  634.1 0.4 convolution_subtract_fusion.2
  634.5 11.7 %cholesky.255 = f32[128,128]{1,0:T(8,128)S(1)} custom-call(f32[128,128]{1,0:T(8,128)S(1)} %convolution_subtract_fusion.2), custom_call_target="Cholesky" | custom-call | tf_op jit(solution)/shard_map/jit(cholesky)/cholesky | solution.py:85
  646.2 0.7 compare_reduce_fusion.1
  646.9 0.6 compare_reduce_fusion
  647.5 0.7 compare_reduce_fusion.2
  650.7 0.1 select_bitcast_fusion
  650.9 1.3 copy.21
  (14 shorter events, 0.2 us)
Async XLA Ops:
  7.9 12.4 %collective-permute-start = (f32[16,512]{1,0:T(8,128)S(1)}, f32[16,512]{1,0:T(8,128)S(1)}, u32[]{:S(2)}, u32[]{:S(2)}) collective-permute-start(f32[16,512]{1,0:T(8,128)S(1)} %get-tuple-element.12), channel_id=1, source_target_pairs={{0,1},{1,2},{2,3},{3,4},{4,5},{5,6},{6,7},{7,8},{8,9},{9,10},{10,1... | collective-permute-start | bytes 98312 | tf_op jit(solution)/shard_map/ppermute | solution.py:12
  12.9 19.5 %collective-permute-start.1 = (f32[16,512]{1,0:T(8,128)S(1)}, f32[16,512]{1,0:T(8,128)S(1)}, u32[]{:S(2)}, u32[]{:S(2)}) collective-permute-start(f32[16,512]{1,0:T(8,128)S(1)} %get-tuple-element.13), channel_id=1, source_target_pairs={{1,0},{2,1},{3,2},{4,3},{5,4},{6,5},{7,6},{8,7},{9,8},{10,9},{11,1... | collective-permute-start | bytes 98312 | tf_op jit(solution)/shard_map/ppermute | solution.py:15
  209.3 188.4 %all-to-all-start = ((f32[32,128,512]{2,1,0:T(8,128)}), f32[32,128,512]{2,1,0:T(8,128)}, u32[]{:S(2)}, u32[]{:S(2)}) async-start(f32[32,128,512]{2,1,0:T(8,128)} %broadcast_select_fusion), calls=%async_computation | async-start | bytes 16777216 | tf_op jit(solution)/shard_map/all_to_all | solution.py:67
  216.3 347.8 %all-reduce.3.cloned.1.call-start = ((), (), s32[]{:S(2)}) async-start(), calls=%async_computation.1 | async-start | bytes 2097152 | tf_op jit(solution)/shard_map/psum | solution.py:84
  427.4 223.5 %copy-start = (f32[256,512]{1,0:T(8,128)}, f32[256,512]{1,0:T(8,128)S(1)}, u32[]{:S(2)}) copy-start(f32[256,512]{1,0:T(8,128)S(1)} %broadcast_select_fusion.1) | copy-start | bytes 1572868
Sparse Core Ops, SparseCore 0:
  429.5 134.5 all-reduce.2
where the time goes:
time: 664 us; the launch traced here: 659 us
  waiting for transfers between devices  315 us (47%)
  other arithmetic  212 us (32%)
  local copies, waits for them, and re-layouts  54.7 us (8%)
  matrix products  47 us (7%)
  between operations  17.3 us (3%)
  starting transfers between devices  13.3 us (2%)
    all_to_all x1, waiting for transfers between devices, on_device(): lax.all_to_all(outgoing, ('tm', 'grp'), split_axis=0, concat_axis=0, tile...  181 us
    psum x1, waiting for transfers between devices, on_device(): gram = lax.psum(local_gram, ('tm', 'grp'))  135 us
    mul x1, other arithmetic, on_device(): flipped = filtered * sign_flips.astype(jnp.float32)[:, None]  123 us
    another operation x14, other arithmetic, on_device(): lower = jnp.linalg.cholesky(gram / sample_count)  78.8 us
    gather x1, local copies, waits for them, and re-layouts, on_device(): outgoing = jnp.take(mixed, used_positions, axis=0)  21.4 us
    dot_general x1, matrix products, on_device(): jnp.einsum('op,pkw->okw', hadamard(devices_all), stacked, precision=lax.P...  16.9 us
    dot_general x1, matrix products, local_transform(): jnp.einsum('vy,uyw->uvw', hadamard(inner), layered, precision=lax.Precisi...  13.8 us
  transfers between devices with their start and end apart: 4, of which 2 were waited for; matrix products, arithmetic and copies ran while one was open for 3% of the time, Pallas kernels for 0%

commit v1 on v0

--- a/solution.py
+++ b/solution.py
@@ -81,7 +81,7 @@
         precision=lax.Precision.HIGHEST,
         preferred_element_type=jnp.float32,
     )
-    gram = lax.psum(local_gram, ("tm", "grp"))
+    gram = jnp.sum(lax.all_gather(local_gram, ("tm", "grp")), axis=0)
     lower = jnp.linalg.cholesky(gram / sample_count)
     return (sketch, lower.T)
 

time: 664 us -> 743 us (1.12)
  waiting for transfers between devices: 315 us -> 379 us
  other arithmetic: 212 us -> 222 us
    all_gather x0 -> x1, waiting for transfers between devices: none -> 198 us  [on_device(): gram = jnp.sum(lax.all_gather(local_gram, ('tm', 'grp')), axis=0)]
    psum x1 -> x0, waiting for transfers between devices: 135 us -> none  [on_device(): gram = lax.psum(local_gram, ('tm', 'grp'))]
    reduce_sum x0 -> x1, other arithmetic: none -> 12.5 us  [on_device(): gram = jnp.sum(lax.all_gather(local_gram, ('tm', 'grp')), axis=0)]
where the time goes in v1:
time: 743 us; the launch traced here: 738 us
  waiting for transfers between devices  379 us (51%)
  other arithmetic  222 us (30%)
  local copies, waits for them, and re-layouts  55.7 us (7%)
  matrix products  50.8 us (7%)
  between operations  17.3 us (2%)
  starting transfers between devices  13.3 us (2%)
    all_gather x1, waiting for transfers between devices, on_device(): gram = jnp.sum(lax.all_gather(local_gram, ('tm', 'grp')), axis=0)  198 us
    all_to_all x1, waiting for transfers between devices, on_device(): lax.all_to_all(outgoing, ('tm', 'grp'), split_axis=0, concat_axis=0, tile...  181 us
    mul x1, other arithmetic, on_device(): flipped = filtered * sign_flips.astype(jnp.float32)[:, None]  123 us
    another operation x14, other arithmetic, on_device(): lower = jnp.linalg.cholesky(gram / sample_count)  78.7 us
    gather x1, local copies, waits for them, and re-layouts, on_device(): outgoing = jnp.take(mixed, used_positions, axis=0)  21.4 us
    dot_general x1, matrix products, on_device(): jnp.einsum('op,pkw->okw', hadamard(devices_all), stacked, precision=lax.P...  17.3 us
  transfers between devices with their start and end apart: 4, of which 2 were waited for; matrix products, arithmetic and copies ran while one was open for 3% of the time, Pallas kernels for 0%

profile of v1, /device:TPU:0, one launch (start us, length us, event | category | flops | bytes accessed | tf_op | source)
XLA Modules:
  0.0 737.6 jit_solution(364526677447432609)
XLA Ops:
  7.2 0.8 fusion.110
  7.9 4.9 collective-permute-start
  12.9 1.3 collective-permute-start.1
  14.2 1.4 slice.317
  15.6 2.1 fusion.111
  17.7 1.9 fusion.112
  19.6 0.7 convert_element_type.14
  20.3 0.6 constant_dynamic-update-slice_fusion.1
  20.9 11.5 %constant_dynamic-update-slice_fusion = (f32[4112,512]{1,0:T(8,128)}, f32[4112,512]{1,0:T(8,128)}) fusion(f32[4112,512]{1,0:T(8,128)} %constant_dynamic-update-slice_fusion.1, f32[4096,512]{1,0:T(8,128)} %param.4), kind=kLoop, calls=%fused_computation.142 | loop fusion | bytes 25165824 | tf_op jit(solution)/shard_map/concatenate | solution.py:16
  32.4 0.6 constant_dynamic-update-slice_fusion.2
  33.0 122.9 %fusion.1 = f32[4096,512]{1,0:T(8,128)S(1)} fusion(f32[4112,512]{1,0:T(8,128)} %constant_dynamic-update-slice_fusion.2, f32[4112,512]{1,0:T(8,128)} %get-tuple-element.10, f32[4096,512]{1,0:T(8,128)} %param.4, f32[4096]{0:T(1024)S(1)} %convert_element_type.14, f32[]{:T(128)} %bitcast.35, f32[]{:T(128)} %bitcast.34, f32[]{:T(128)} %bitcast.33, f32[]{:T(128)} %bitcast.32, ...), kind=kLoop, calls=%fused_computation.4 | loop fusion | flops 138412032 | bytes 285229184 | tf_op jit(solution)/shard_map/mul | solution.py:57
  156.0 12.4 %fusion.37 = f32[64,64,512]{2,0,1:T(8,128)S(1)} fusion(f32[64,64,512]{2,1,0:T(8,128)S(1)} %bitcast.78), kind=kOutput, calls=%fused_computation.71 | convolution fusion | flops 1610715136 | bytes 16777216 | tf_op jit(solution)/shard_map/ux,xvw->uvw/dot_general | solution.py:40
  168.4 13.6 %fusion.35 = f32[64,512,64]{1,2,0:T(8,128)} fusion(f32[64,64,512]{2,0,1:T(8,128)S(1)} %fusion.37), kind=kOutput, calls=%fused_computation.69 | convolution fusion | flops 1610715136 | bytes 16777216 | tf_op jit(solution)/shard_map/vy,uyw->uvw/dot_general | solution.py:41
  182.0 21.4 %gather_fusion = f32[4096,512]{1,0:T(8,128)} fusion(f32[4096,512]{1,0:T(8,128)} %bitcast.76, s32[4096]{0:T(1024)S(1)} %broadcast_clamp_fusion), kind=kCustom, calls=%fused_computation | custom fusion | bytes 16793600 | tf_op jit(solution)/shard_map/jit(_take)/gather | solution.py:66
  203.4 5.8 broadcast_select_fusion
  209.3 7.0 all-to-all-start
  216.3 0.0 all-gather.3.cloned.1.call-start
  216.3 0.8 compare_and_fusion
  217.1 180.5 %all-to-all-done = f32[32,128,512]{2,1,0:T(8,128)} async-done(((f32[32,128,512]{2,1,0:T(8,128)}), f32[32,128,512]{2,1,0:T(8,128)}, u32[]{:S(2)}, u32[]{:S(2)}) %all-to-all-start) | async-done | bytes 8388640 | tf_op jit(solution)/shard_map/all_to_all | solution.py:67
  397.7 17.3 %broadcast_multiply_fusion = f32[32,128,512]{2,0,1:T(8,128)S(1)} fusion(f32[32,128,512]{2,1,0:T(8,128)} %all-to-all-done), kind=kOutput, calls=%fused_computation.73 | convolution fusion | flops 807426048 | bytes 16777216 | tf_op jit(solution)/shard_map/op,pkw->okw/dot_general | solution.py:70
  415.0 8.1 %copy.16 = f32[32,128,512]{2,1,0:T(8,128)} copy(f32[32,128,512]{2,0,1:T(8,128)S(1)} %broadcast_multiply_fusion) | data formatting | bytes 16777216 | tf_op jit(solution)/shard_map/mul | solution.py:70
  423.1 4.6 gather_fusion.1
  427.7 0.1 broadcast_select_fusion.1
  427.8 2.0 fusion.113
  429.8 198.1 %all-gather.3.cloned.1.call-done = f32[16384,512]{1,0:T(8,128)} async-done(((f32[512,512]{1,0:T(8,128)}), f32[16384,512]{1,0:T(8,128)}) %all-gather.3.cloned.1.call-update) | async-done | bytes 33554448 | tf_op jit(solution)/shard_map/all_gather | solution.py:84
  627.9 12.5 %reduce_sum.11 = f32[512,512]{1,0:T(8,128)S(1)} reduce(f32[32,512,512]{2,1,0:T(8,128)} %bitcast.79, f32[]{:T(128)} %constant.234.clone.1), dimensions={0}, to_apply=%region_0.1 | reduce | flops 8126464 | bytes 34603012 | tf_op jit(solution)/shard_map/reduce_sum | solution.py:84
  640.4 0.3 copy.17
  640.8 0.2 fusion.41
  641.0 1.0 copy-done.1
  642.0 11.7 %cholesky.104 = f32[128,128]{1,0:T(8,128)S(1)} custom-call(f32[128,128]{1,0:T(8,128)S(1)} %cholesky.266), custom_call_target="Cholesky" | custom-call | tf_op jit(solution)/shard_map/jit(cholesky)/cholesky | solution.py:85
  653.7 0.1 cholesky.224
  653.9 9.8 %custom-call.27 = f32[1,128,128]{1,2,0:T(8,128)S(1)} custom-call(f32[1,128,128]{2,1,0:T(8,128)S(1)} %get-tuple-element.23), custom_call_target="InvertDiagBlocksLowerTriangular" | custom-call | tf_op jit(solution)/shard_map/jit(cholesky)/cholesky | solution.py:85
  663.7 1.2 constant_dynamic-update-slice_fusion.6
  664.9 1.3 convolution_subtract_fusion
  666.2 11.7 %cholesky.217 = f32[128,128]{1,0:T(8,128)S(1)} custom-call(f32[128,128]{1,0:T(8,128)S(1)} %cholesky.270), custom_call_target="Cholesky" | custom-call | tf_op jit(solution)/shard_map/jit(cholesky)/cholesky | solution.py:85
  677.9 10.0 %custom-call.28 = f32[1,128,128]{1,2,0:T(8,128)S(1)} custom-call(f32[1,128,128]{2,1,0:T(8,128)S(1)} %get-tuple-element.20), custom_call_target="InvertDiagBlocksLowerTriangular" | custom-call | tf_op jit(solution)/shard_map/jit(cholesky)/cholesky | solution.py:85
  688.0 0.3 convolution_dynamic-update-slice_fusion
  688.3 1.3 convolution_subtract_fusion.1
  689.6 11.7 %cholesky.238 = f32[128,128]{1,0:T(8,128)S(1)} custom-call(f32[128,128]{1,0:T(8,128)S(1)} %cholesky.275), custom_call_target="Cholesky" | custom-call | tf_op jit(solution)/shard_map/jit(cholesky)/cholesky | solution.py:85
  701.3 0.7 compare_reduce_fusion.1
  702.0 9.8 %custom-call.29 = f32[1,128,128]{1,2,0:T(8,128)S(1)} custom-call(f32[1,128,128]{2,1,0:T(8,128)S(1)} %get-tuple-element.17), custom_call_target="InvertDiagBlocksLowerTriangular" | custom-call | tf_op jit(solution)/shard_map/jit(cholesky)/cholesky | solution.py:85
  711.8 0.2 convolution_dynamic-update-slice_fusion.1
  712.1 1.2 convolution_subtract_fusion.2
  713.3 11.7 %cholesky.255 = f32[128,128]{1,0:T(8,128)S(1)} custom-call(f32[128,128]{1,0:T(8,128)S(1)} %convolution_subtract_fusion.2), custom_call_target="Cholesky" | custom-call | tf_op jit(solution)/shard_map/jit(cholesky)/cholesky | solution.py:85
  725.0 0.6 compare_reduce_fusion
  725.7 0.7 compare_reduce_fusion.2
  728.9 0.1 select_bitcast_fusion
  729.0 1.3 copy.18
  (16 shorter events, 0.2 us)
Async XLA Ops:
  7.9 12.4 %collective-permute-start = (f32[16,512]{1,0:T(8,128)S(1)}, f32[16,512]{1,0:T(8,128)S(1)}, u32[]{:S(2)}, u32[]{:S(2)}) collective-permute-start(f32[16,512]{1,0:T(8,128)S(1)} %get-tuple-element.12), channel_id=1, source_target_pairs={{0,1},{1,2},{2,3},{3,4},{4,5},{5,6},{6,7},{7,8},{8,9},{9,10},{10,1... | collective-permute-start | bytes 98312 | tf_op jit(solution)/shard_map/ppermute | solution.py:12
  12.9 19.5 %collective-permute-start.1 = (f32[16,512]{1,0:T(8,128)S(1)}, f32[16,512]{1,0:T(8,128)S(1)}, u32[]{:S(2)}, u32[]{:S(2)}) collective-permute-start(f32[16,512]{1,0:T(8,128)S(1)} %get-tuple-element.13), channel_id=1, source_target_pairs={{1,0},{2,1},{3,2},{4,3},{5,4},{6,5},{7,6},{8,7},{9,8},{10,9},{11,1... | collective-permute-start | bytes 98312 | tf_op jit(solution)/shard_map/ppermute | solution.py:15
  209.3 188.4 %all-to-all-start = ((f32[32,128,512]{2,1,0:T(8,128)}), f32[32,128,512]{2,1,0:T(8,128)}, u32[]{:S(2)}, u32[]{:S(2)}) async-start(f32[32,128,512]{2,1,0:T(8,128)} %broadcast_select_fusion), calls=%async_computation | async-start | bytes 16777216 | tf_op jit(solution)/shard_map/all_to_all | solution.py:67
  216.3 411.6 %all-gather.3.cloned.1.call-start = ((), (), s32[]{:S(2)}) async-start(), calls=%async_computation.1 | async-start | bytes 34603008 | tf_op jit(solution)/shard_map/all_gather | solution.py:84
  427.8 212.7 %copy-start = (f32[256,512]{1,0:T(8,128)}, f32[256,512]{1,0:T(8,128)S(1)}, u32[]{:S(2)}) copy-start(f32[256,512]{1,0:T(8,128)S(1)} %broadcast_select_fusion.1) | copy-start | bytes 1572868
  641.0 1.0 copy-start.1
Sparse Core Ops, SparseCore 0:
  429.9 197.9 all-gather.2
